TPU v7x, 32 devices: a whole 2x2x4 slice. The times are simulated.
32 devices in a mesh: blk: 4 (over z), virt: 8 (over y, x, core).
Axes of the slice: x: 2, y: 2, z: 4, core: 2. Of those that a mesh axis runs over, the one named last changes fastest.
Arguments:
- integrals: bfloat16 [512, 16, 4096], P(('blk', 'virt')), may hold values from -0.09375 to 0.09375
- amplitudes: bfloat16 [256, 4096], P('blk'), may hold values from -6 to 6
- readers: int32 [512], P(('blk', 'virt')), may hold values from 0 to 7, as said below
- row_slots: int32 [512], P(('blk', 'virt')), may hold values from 0 to 3
- tile_mask: int32 [512, 4], P(('blk', 'virt')), may hold values 0 or 1
- virt_energy: float32 [2048], P(('blk', 'virt')), may hold values from 1 to 3
- occ_energy: float32 [1200], replicated, may hold values from -1 to -0.25
- pair_first: int32 [256], replicated, may hold values from 0 to 1199
- pair_second: int32 [256], replicated, may hold values from 0 to 1199
Outputs:
- update: bfloat16 [2048, 256], P(('blk', 'virt'))
Inputs may be any that keep to these rules, and one draw needn't show every extreme that they name: `readers`: each tile names a reader on the virt axis in the same blk row as its generating device; one device names one reader at most 4 times, and in every blk row some reader is named 4 times by every device of that row.
All inputs are finite; a program needn't handle non-finite values. No bound on the sum of `tile_mask` on one device may be relied on, other than what follows from the above.
Results may differ from a plain program's by a relative error of at most 0.001.
Values may be sent and summed in bfloat16 or wider, within the bound.
A program may use at most 64 MiB of HBM per device.

v0:
```python
import jax
import jax.numpy as jnp
from jax import lax
from jax.sharding import PartitionSpec as P


def body(
    integrals,
    amplitudes,
    readers,
    row_slots,
    tile_mask,
    virt_energy,
    occ_energy,
    pair_first,
    pair_second,
):
    virt_count = lax.axis_size("virt")
    blk_count = lax.axis_size("blk")
    generated = integrals.shape[0]
    tile_rows = integrals.shape[1]
    panel_rows = amplitudes.shape[0]
    capacity = max(1, 2 * generated // virt_count)
    slot_count = virt_count * capacity
    row_blocks = virt_energy.shape[0] // tile_rows
    tile_order = jnp.arange(generated, dtype=jnp.int32)
    same_reader = readers[:, None] == readers[None, :]
    earlier = tile_order[None, :] < tile_order[:, None]
    within = jnp.sum((same_reader & earlier).astype(jnp.int32), axis=1)
    position = readers * capacity + within
    placing = jnp.arange(slot_count, dtype=jnp.int32)[:, None] == position[None, :]
    filled = jnp.any(placing, axis=1)
    source_tile = jnp.sum(placing.astype(jnp.int32) * tile_order[None, :], axis=1)
    row_hot = (row_slots[:, None] == jnp.arange(row_blocks, dtype=jnp.int32)[None, :]).astype(
        jnp.float32
    )
    mask_float = tile_mask.astype(jnp.float32)
    sent_tiles = jnp.where(
        filled[:, None, None], integrals[source_tile], jnp.zeros((), jnp.bfloat16)
    )
    coefficient = (row_hot[:, :, None] * mask_float[:, None, :]).reshape(
        generated, row_blocks * blk_count
    )
    sent_coef = jnp.where(filled[:, None], coefficient[source_tile], 0.0).astype(jnp.bfloat16)
    got_tiles, got_coef = (
        lax.all_to_all(sent_tiles, "virt", split_axis=0, concat_axis=0, tiled=True),
        lax.all_to_all(sent_coef, "virt", split_axis=0, concat_axis=0, tiled=True),
    )
    got_coef = got_coef.astype(jnp.float32).reshape(slot_count, row_blocks, blk_count)
    panel = lax.all_gather(amplitudes, "blk", axis=0, tiled=True)
    column_count = panel.shape[0]
    column_panel = jnp.arange(column_count, dtype=jnp.int32) // panel_rows
    columns = jnp.einsum(
        "srk,kp->srp",
        got_coef,
        (jnp.arange(blk_count, dtype=jnp.int32)[:, None] == column_panel[None, :]).astype(
            jnp.float32
        ),
        precision=lax.Precision.HIGHEST,
    )
    product = jnp.einsum("stw,pw->stp", got_tiles, panel, preferred_element_type=jnp.float32)
    summed_panel = jnp.einsum("srp,stp->rtp", columns, product, precision=lax.Precision.HIGHEST)
    summed = summed_panel.reshape(row_blocks * tile_rows, column_count)
    levels = jnp.arange(occ_energy.shape[0], dtype=jnp.int32)[None, :]
    first_energy = jnp.sum(
        jnp.where(pair_first[:, None] == levels, occ_energy[None, :], 0.0), axis=1
    )
    second_energy = jnp.sum(
        jnp.where(pair_second[:, None] == levels, occ_energy[None, :], 0.0), axis=1
    )
    denominator = virt_energy[:, None] - first_energy[None, :] - second_energy[None, :]
    return (summed / denominator).astype(jnp.bfloat16)


def solution(mesh):
    placed = (
        P(("blk", "virt"), None, None),
        P("blk", None),
        P(("blk", "virt")),
        P(("blk", "virt")),
        P(("blk", "virt"), None),
        P(("blk", "virt")),
        P(),
        P(),
        P(),
    )
    return jax.shard_map(
        body, mesh=mesh, in_specs=placed, out_specs=P(("blk", "virt"), None), check_vma=False
    )
```

profile of v0, /device:TPU:0, one launch (start us, length us, event | category | flops | bytes accessed | tf_op | source)
XLA Modules:
  0.0 97.9 jit_solution(15406979760878977125)
XLA Ops:
  6.5 0.0 copy-start
  6.5 1.0 %convert_reduce_fusion = s32[16]{0:T(128)S(1)} fusion(s32[16]{0:T(128)} %param.11), kind=kLoop, calls=%fused_computation.16 | loop fusion | flops 1264 | bytes 128 | tf_op jit(solution)/shard_map/reduce_sum | solution.py:29
  7.5 0.7 multiply_add_fusion
  8.2 0.1 select_reduce_fusion.2
  8.3 0.1 fusion.5
  8.4 0.7 convert_element_type.25
  9.1 0.7 fusion.10
  9.8 0.1 copy.20
  9.8 0.1 broadcast_in_dim.44
  9.9 0.6 gather_fusion.1
  10.5 0.7 select_convert_fusion
  11.2 5.2 %all-to-all-start.1 = ((bf16[8,4,16]{2,1,0:T(4,128)(2,1)}), bf16[8,4,16]{2,1,0:T(4,128)(2,1)S(1)}, u32[]{:S(2)}, u32[]{:S(2)}) async-start(bf16[8,4,16]{2,1,0:T(4,128)(2,1)} %select_convert_fusion), calls=%async_computation.1 | async-start | bytes 16384 | tf_op jit(solution)/shard_map/all_to_all | solution.py:47
  16.4 0.0 copy-done
  16.4 2.8 %gather_fusion = bf16[32,16,4096]{2,1,0:T(8,128)(2,1)} fusion(bf16[16,16,4096]{2,1,0:T(8,128)(2,1)S(1)} %copy-done, s32[1024]{0:T(1024)S(1)} %pad_clamp_fusion), kind=kCustom, calls=%fused_computation | custom fusion | bytes 8388736 | tf_op jit(solution)/shard_map/gather | solution.py:39
  19.2 4.5 %broadcast_select_fusion = bf16[32,16,4096]{2,1,0:T(8,128)(2,1)} fusion(bf16[32,16,4096]{2,1,0:T(8,128)(2,1)} %gather_fusion, pred[32]{0:T(512)(128)(4,1)S(1)} %fusion.5), kind=kLoop, calls=%fused_computation.2 | loop fusion | flops 2097152 | bytes 8388640 | tf_op jit(solution)/shard_map/jit(_where)/select_n | solution.py:38
  23.7 0.0 all-to-all-done.1
  23.7 4.7 %all-to-all-start = ((bf16[32,16,4096]{2,1,0:T(8,128)(2,1)}), bf16[32,16,4096]{2,1,0:T(8,128)(2,1)}, u32[]{:S(2)}, u32[]{:S(2)}) async-start(bf16[32,16,4096]{2,1,0:T(8,128)(2,1)} %broadcast_select_fusion), calls=%async_computation | async-start | bytes 8388608 | tf_op jit(solution)/shard_map/all_to_all | solution.py:46
  28.4 0.0 all-gather.2.cloned.1.call-start
  28.4 0.7 all-gather.2.cloned.1.call-update
  29.1 0.0 copy-done.1
  29.1 0.0 copy-done.2
  29.2 0.4 select_reduce_fusion.1
  29.5 0.1 reshape.99
  29.6 0.1 fusion.3
  29.8 0.2 copy.23
  30.0 48.4 %all-gather.2.cloned.1.call-done = bf16[256,4096]{1,0:T(8,128)(2,1)} async-done(((bf16[64,4096]{1,0:T(8,128)(2,1)}), bf16[256,4096]{1,0:T(8,128)(2,1)}) %all-gather.2.cloned.1.call-update) | async-done | bytes 2097168 | tf_op jit(solution)/shard_map/all_gather | solution.py:50
  78.4 0.0 all-to-all-done
  78.4 4.1 %fusion = f32[32,16,256]{2,1,0:T(8,128)S(1)} fusion(bf16[32,16,4096]{2,1,0:T(8,128)(2,1)} %all-to-all-done, bf16[256,4096]{1,0:T(8,128)(2,1)} %all-gather.2.cloned.1.call-done), kind=kOutput, calls=%fused_computation.3 | convolution fusion | flops 1073741824 | bytes 6815744 | tf_op jit(solution)/shard_map/stw,pw->stp/dot_general | solution.py:61
  82.6 2.6 %copy.22 = f32[32,16,256]{0,1,2:T(8,128)} copy(f32[32,16,256]{2,1,0:T(8,128)S(1)} %fusion) | data formatting | bytes 1048576 | tf_op jit(solution)/shard_map/stw,pw->stp/dot_general | solution.py:61
  85.2 5.0 %convolution_bitcast_fusion = f32[4,16,256]{1,0,2:T(4,128)S(1)} fusion(f32[32,16,256]{0,1,2:T(8,128)} %copy.22, f32[32,4,256]{0,1,2:T(4,128)S(1)} %copy.23), kind=kOutput, calls=%fused_computation.5 | convolution fusion | flops 6291456 | bytes 720896 | tf_op jit(solution)/shard_map/srp,stp->rtp/dot_general | solution.py:62
  90.2 0.2 copy.24
  90.4 0.7 fusion.2
  (10 shorter events, 0.0 us)
Async XLA Ops:
  6.5 9.8 %copy-start = (bf16[16,16,4096]{2,1,0:T(8,128)(2,1)S(1)}, bf16[16,16,4096]{2,1,0:T(8,128)(2,1)}, u32[]{:S(2)}) copy-start(bf16[16,16,4096]{2,1,0:T(8,128)(2,1)} %param.9) | copy-start | bytes 6291460
  11.2 12.5 %all-to-all-start.1 = ((bf16[8,4,16]{2,1,0:T(4,128)(2,1)}), bf16[8,4,16]{2,1,0:T(4,128)(2,1)S(1)}, u32[]{:S(2)}, u32[]{:S(2)}) async-start(bf16[8,4,16]{2,1,0:T(4,128)(2,1)} %select_convert_fusion), calls=%async_computation.1 | async-start | bytes 16384 | tf_op jit(solution)/shard_map/all_to_all | solution.py:47
  23.7 5.5 %copy-start.1 = (f32[1200]{0:T(1024)S(1)}, f32[1200]{0:T(1024)}, u32[]{:S(2)}) copy-start(f32[1200]{0:T(1024)} %param.15) | copy-start | bytes 14404
  23.7 5.5 %copy-start.2 = (s32[256]{0:T(256)S(1)}, s32[256]{0:T(256)}, u32[]{:S(2)}) copy-start(s32[256]{0:T(256)} %param.16) | copy-start | bytes 3076
  23.7 5.5 %copy-start.3 = (s32[256]{0:T(256)S(1)}, s32[256]{0:T(256)}, u32[]{:S(2)}) copy-start(s32[256]{0:T(256)} %param.17) | copy-start | bytes 3076
  23.7 54.8 %all-to-all-start = ((bf16[32,16,4096]{2,1,0:T(8,128)(2,1)}), bf16[32,16,4096]{2,1,0:T(8,128)(2,1)}, u32[]{:S(2)}, u32[]{:S(2)}) async-start(bf16[32,16,4096]{2,1,0:T(8,128)(2,1)} %broadcast_select_fusion), calls=%async_computation | async-start | bytes 8388608 | tf_op jit(solution)/shard_map/all_to_all | solution.py:46
  28.4 50.1 %all-gather.2.cloned.1.call-start = ((), (), s32[]{:S(2)}) async-start(), calls=%async_computation.2 | async-start | bytes 2621440 | tf_op jit(solution)/shard_map/all_gather | solution.py:50
  85.2 5.2 %copy-start.4 = (f32[64]{0:T(128)S(1)}, f32[64]{0:T(128)}, u32[]{:S(2)}) copy-start(f32[64]{0:T(128)} %param.14) | copy-start | bytes 772
Sparse Core Ops, SparseCore 0:
  30.8 47.6 all-gather.1
where the time goes:
time: 98.4 us; the launch traced here: 97.9 us
  waiting for transfers between devices  49.1 us (50%)
  between operations  13.5 us (14%)
  starting transfers between devices  9.9 us (10%)
  other arithmetic  9.47 us (10%)
  matrix products  9.28 us (9%)
  local copies, waits for them, and re-layouts  6.7 us (7%)
    all_gather x1, waiting for transfers between devices, body(): panel = lax.all_gather(amplitudes, 'blk', axis=0, tiled=True)  48.4 us
    all_to_all x1, starting transfers between devices, body(): lax.all_to_all(sent_coef, 'virt', split_axis=0, concat_axis=0, tiled=True)  5.17 us
    dot_general x1, matrix products, body(): jnp.einsum('srp,stp->rtp', columns, product, precision=lax.Precision.HIGH...  4.99 us
    all_to_all x1, starting transfers between devices, body(): lax.all_to_all(sent_tiles, 'virt', split_axis=0, concat_axis=0, tiled=True)  4.69 us
    select_n x1, other arithmetic, body(): jnp.where(filled[:, None, None], integrals[source_tile], jnp.zeros((), jn...  4.5 us
    dot_general x1, matrix products, body(): jnp.einsum('stw,pw->stp', got_tiles, panel, preferred_element_type=jnp.fl...  4.15 us
    gather x1, local copies, waits for them, and re-layouts, body(): integrals[source_tile]  2.79 us
    dot_general x1, local copies, waits for them, and re-layouts, body(): jnp.einsum('stw,pw->stp', got_tiles, panel, preferred_element_type=jnp.fl...  2.62 us
  transfers between devices with their start and end apart: 3, of which 1 were waited for; matrix products, arithmetic and copies ran while one was open for 8% of the time, Pallas kernels for 0%

commit v1 on v0

--- a/solution.py
+++ b/solution.py
@@ -47,7 +47,21 @@
         lax.all_to_all(sent_coef, "virt", split_axis=0, concat_axis=0, tiled=True),
     )
     got_coef = got_coef.astype(jnp.float32).reshape(slot_count, row_blocks, blk_count)
-    panel = lax.all_gather(amplitudes, "blk", axis=0, tiled=True)
+    ways, here, step = (lax.axis_size("blk"), lax.axis_index("blk"), amplitudes.shape[0])
+    lengths = [n * ways if d == 0 else n for d, n in enumerate(amplitudes.shape)]
+    full = lax.dynamic_update_slice_in_dim(
+        jnp.zeros(lengths, amplitudes.dtype), amplitudes, here * step, axis=0
+    )
+    going_up = going_down = amplitudes
+    for far in range(1, ways // 2 + 1):
+        going_up = lax.ppermute(going_up, "blk", [(d, (d + 1) % ways) for d in range(ways)])
+        full = lax.dynamic_update_slice_in_dim(full, going_up, (here - far) % ways * step, axis=0)
+        if 2 * far < ways:
+            going_down = lax.ppermute(going_down, "blk", [(d, (d - 1) % ways) for d in range(ways)])
+            full = lax.dynamic_update_slice_in_dim(
+                full, going_down, (here + far) % ways * step, axis=0
+            )
+    panel = full
     column_count = panel.shape[0]
     column_panel = jnp.arange(column_count, dtype=jnp.int32) // panel_rows
     columns = jnp.einsum(

time: 98.4 us -> 84.1 us (0.85)
  between operations: 13.5 us -> 0.1 us
  waiting for transfers between devices: 49.1 us -> 37.2 us
  local copies, waits for them, and re-layouts: 6.7 us -> 13.9 us
  starting transfers between devices: 9.9 us -> 13.7 us
    all_gather x1 -> x0, waiting for transfers between devices: 48.4 us -> none  [body(): panel = lax.all_gather(amplitudes, 'blk', axis=0, tiled=True)]
    ppermute x0 -> x3, waiting for transfers between devices: none -> 27.6 us  [the longest x2 19.3 us: body(): lax.ppermute(going_up, 'blk', [(d, (d + 1) % ways) for d in range(ways)])]
    all_to_all x1, waiting for transfers between devices: 0.01 us -> 9.53 us  [body(): lax.all_to_all(sent_tiles, 'virt', split_axis=0, concat_axis=0, tiled=True)]
    dynamic_update_slice x0 -> x4, local copies, waits for them, and re-layouts: none -> 5.55 us  [the longest x2 2.73 us: body(): lax.dynamic_update_slice_in_dim(full, going_up, (here - far) % ways * ste...]
    ppermute x0 -> x3, starting transfers between devices: none -> 3.88 us  [the longest x1 2.25 us: body(): lax.ppermute(going_down, 'blk', [(d, (d - 1) % ways) for d in range(ways)])]
    broadcast_in_dim x0 -> x1, local copies, waits for them, and re-layouts: none -> 1.63 us  [body(): jnp.zeros(lengths, amplitudes.dtype)]
  transfers between devices with their start and end apart: 3 -> 5, of which waited for: 1 -> 4; matrix products, arithmetic and copies ran while one was open for 8% -> 18% of each run, Pallas kernels for 0% -> 0%
where the time goes in v1:
time: 84.1 us; the launch traced here: 83.6 us
  waiting for transfers between devices  37.2 us (44%)
  local copies, waits for them, and re-layouts  13.9 us (17%)
  starting transfers between devices  13.7 us (16%)
  other arithmetic  9.47 us (11%)
  matrix products  9.28 us (11%)
    ppermute x2, waiting for transfers between devices, body(): lax.ppermute(going_up, 'blk', [(d, (d + 1) % ways) for d in range(ways)])  19.3 us
    all_to_all x1, waiting for transfers between devices, body(): lax.all_to_all(sent_tiles, 'virt', split_axis=0, concat_axis=0, tiled=True)  9.53 us
    ppermute x1, waiting for transfers between devices, body(): lax.ppermute(going_down, 'blk', [(d, (d - 1) % ways) for d in range(ways)])  8.37 us
    all_to_all x1, starting transfers between devices, body(): lax.all_to_all(sent_coef, 'virt', split_axis=0, concat_axis=0, tiled=True)  5.17 us
    dot_general x1, matrix products, body(): jnp.einsum('srp,stp->rtp', columns, product, precision=lax.Precision.HIGH...  4.99 us
    all_to_all x1, starting transfers between devices, body(): lax.all_to_all(sent_tiles, 'virt', split_axis=0, concat_axis=0, tiled=True)  4.68 us
    select_n x1, other arithmetic, body(): jnp.where(filled[:, None, None], integrals[source_tile], jnp.zeros((), jn...  4.5 us
    dot_general x1, matrix products, body(): jnp.einsum('stw,pw->stp', got_tiles, panel, preferred_element_type=jnp.fl...  4.15 us
  transfers between devices with their start and end apart: 5, of which 4 were waited for; matrix products, arithmetic and copies ran while one was open for 18% of the time, Pallas kernels for 0%

profile of v1, /device:TPU:0, one launch (start us, length us, event | category | flops | bytes accessed | tf_op | source)
XLA Modules:
  0.0 83.6 jit_solution(344246022727164185)
XLA Ops:
  0.0 1.0 %convert_reduce_fusion = s32[16]{0:T(128)S(1)} fusion(s32[16]{0:T(128)} %param.11), kind=kLoop, calls=%fused_computation.16 | loop fusion | flops 1264 | bytes 128 | tf_op jit(solution)/shard_map/reduce_sum | solution.py:29
  1.0 0.7 multiply_add_fusion
  1.7 0.1 select_reduce_fusion.2
  1.8 0.1 fusion.5
  1.9 0.7 convert_element_type.25
  2.6 0.7 fusion.10
  3.3 0.1 broadcast_in_dim.47
  3.4 0.6 gather_fusion.1
  4.0 0.7 select_convert_fusion
  4.7 5.2 %all-to-all-start.1 = ((bf16[8,4,16]{2,1,0:T(4,128)(2,1)}), bf16[8,4,16]{2,1,0:T(4,128)(2,1)S(1)}, u32[]{:S(2)}, u32[]{:S(2)}) async-start(bf16[8,4,16]{2,1,0:T(4,128)(2,1)} %select_convert_fusion), calls=%async_computation.1 | async-start | bytes 16384 | tf_op jit(solution)/shard_map/all_to_all | solution.py:47
  9.8 2.8 %gather_fusion = bf16[32,16,4096]{2,1,0:T(8,128)(2,1)} fusion(bf16[16,16,4096]{2,1,0:T(8,128)(2,1)S(1)} %copy-done, s32[1024]{0:T(1024)S(1)} %pad_clamp_fusion), kind=kCustom, calls=%fused_computation | custom fusion | bytes 8388736 | tf_op jit(solution)/shard_map/gather | solution.py:39
  12.6 4.5 %broadcast_select_fusion = bf16[32,16,4096]{2,1,0:T(8,128)(2,1)} fusion(bf16[32,16,4096]{2,1,0:T(8,128)(2,1)} %gather_fusion, pred[32]{0:T(512)(128)(4,1)S(1)} %fusion.5), kind=kLoop, calls=%fused_computation.2 | loop fusion | flops 2097152 | bytes 8388640 | tf_op jit(solution)/shard_map/jit(_where)/select_n | solution.py:38
  17.1 4.7 %all-to-all-start = ((bf16[32,16,4096]{2,1,0:T(8,128)(2,1)}), bf16[32,16,4096]{2,1,0:T(8,128)(2,1)}, u32[]{:S(2)}, u32[]{:S(2)}) async-start(bf16[32,16,4096]{2,1,0:T(8,128)(2,1)} %broadcast_select_fusion), calls=%async_computation | async-start | bytes 8388608 | tf_op jit(solution)/shard_map/all_to_all | solution.py:46
  21.9 1.6 %collective-permute-start = (bf16[64,4096]{1,0:T(8,128)(2,1)S(1)}, bf16[64,4096]{1,0:T(8,128)(2,1)}, u32[]{:S(2)}, u32[]{:S(2)}) collective-permute-start(bf16[64,4096]{1,0:T(8,128)(2,1)S(1)} %copy-done.1), channel_id=1, source_target_pairs={{0,8},{8,16},{16,24},{24,0},{1,9},{9,17},{17,25},{25,1},{2,10},{10... | collective-permute-start | bytes 1572872 | tf_op jit(solution)/shard_map/ppermute | solution.py:57
  23.5 2.2 %collective-permute-start.1 = (bf16[64,4096]{1,0:T(8,128)(2,1)S(1)}, bf16[64,4096]{1,0:T(8,128)(2,1)}, u32[]{:S(2)}, u32[]{:S(2)}) collective-permute-start(bf16[64,4096]{1,0:T(8,128)(2,1)S(1)} %copy-done.1), channel_id=1, source_target_pairs={{0,24},{8,0},{16,8},{24,16},{1,25},{9,1},{17,9},{25,17},{2,26},{10... | collective-permute-start | bytes 1572872 | tf_op jit(solution)/shard_map/ppermute | solution.py:60
  25.7 1.6 %broadcast_in_dim.46 = bf16[256,4096]{1,0:T(8,128)(2,1)} broadcast(bf16[]{:T(256)} %constant.53.clone.1), dimensions={} | broadcast | bytes 2097154 | tf_op jit(solution)/shard_map/broadcast_in_dim | solution.py:53
  27.4 0.9 %constant_dynamic-update-slice_fusion.3 = bf16[256,4096]{1,0:T(8,128)(2,1)} fusion(bf16[256,4096]{1,0:T(8,128)(2,1)} %broadcast_in_dim.46, bf16[64,4096]{1,0:T(8,128)(2,1)S(1)} %copy-done.1, s32[]{:T(128)S(6)} %select_n.65), kind=kLoop, calls=%fused_computation.36 | loop fusion | bytes 1048580 | tf_op jit(solution)/shard_map/dynamic_update_slice | solution.py:52
  28.3 0.4 select_reduce_fusion.1
  28.7 0.1 fusion.3
  28.9 0.2 copy.23
  29.1 9.5 %collective-permute-done = bf16[64,4096]{1,0:T(8,128)(2,1)} collective-permute-done((bf16[64,4096]{1,0:T(8,128)(2,1)S(1)}, bf16[64,4096]{1,0:T(8,128)(2,1)}, u32[]{:S(2)}, u32[]{:S(2)}) %collective-permute-start) | collective-permute-done | bytes 524320 | tf_op jit(solution)/shard_map/ppermute | solution.py:57
  38.6 1.9 %constant_dynamic-update-slice_fusion.2 = bf16[256,4096]{1,0:T(8,128)(2,1)} fusion(bf16[256,4096]{1,0:T(8,128)(2,1)} %constant_dynamic-update-slice_fusion.3, bf16[64,4096]{1,0:T(8,128)(2,1)} %collective-permute-done, s32[]{:T(128)S(6)} %select_n.67), kind=kLoop, calls=%fused_computation.35 | loop fusion | bytes 1048580 | tf_op jit(solution)/shard_map/dynamic_update_slice | solution.py:58
  40.5 8.4 %collective-permute-done.1 = bf16[64,4096]{1,0:T(8,128)(2,1)} collective-permute-done((bf16[64,4096]{1,0:T(8,128)(2,1)S(1)}, bf16[64,4096]{1,0:T(8,128)(2,1)}, u32[]{:S(2)}, u32[]{:S(2)}) %collective-permute-start.1) | collective-permute-done | bytes 524320 | tf_op jit(solution)/shard_map/ppermute | solution.py:60
  48.9 1.9 %constant_dynamic-update-slice_fusion.1 = bf16[256,4096]{1,0:T(8,128)(2,1)} fusion(bf16[256,4096]{1,0:T(8,128)(2,1)} %constant_dynamic-update-slice_fusion.2, bf16[64,4096]{1,0:T(8,128)(2,1)} %collective-permute-done.1, s32[]{:T(128)S(6)} %select_n.69), kind=kLoop, calls=%fused_computation.34 | loop fusion | bytes 1048580 | tf_op jit(solution)/shard_map/dynamic_update_slice | solution.py:61
  50.8 9.8 %collective-permute-done.2 = bf16[64,4096]{1,0:T(8,128)(2,1)S(1)} collective-permute-done((bf16[64,4096]{1,0:T(8,128)(2,1)}, bf16[64,4096]{1,0:T(8,128)(2,1)S(1)}, u32[]{:S(2)}, u32[]{:S(2)}) %collective-permute-start.2) | collective-permute-done | bytes 524320 | tf_op jit(solution)/shard_map/ppermute | solution.py:57
  60.6 0.8 constant_dynamic-update-slice_fusion
  61.4 9.5 %all-to-all-done = bf16[32,16,4096]{2,1,0:T(8,128)(2,1)} async-done(((bf16[32,16,4096]{2,1,0:T(8,128)(2,1)}), bf16[32,16,4096]{2,1,0:T(8,128)(2,1)}, u32[]{:S(2)}, u32[]{:S(2)}) %all-to-all-start) | async-done | bytes 4194336 | tf_op jit(solution)/shard_map/all_to_all | solution.py:46
  71.0 4.1 %fusion = f32[32,16,256]{2,1,0:T(8,128)S(1)} fusion(bf16[32,16,4096]{2,1,0:T(8,128)(2,1)} %all-to-all-done, bf16[256,4096]{1,0:T(8,128)(2,1)} %constant_dynamic-update-slice_fusion), kind=kOutput, calls=%fused_computation.3 | convolution fusion | flops 1073741824 | bytes 6815744 | tf_op jit(solution)/shard_map/stw,pw->stp/dot_general | solution.py:75
  75.1 2.6 %copy.22 = f32[32,16,256]{0,1,2:T(8,128)} copy(f32[32,16,256]{2,1,0:T(8,128)S(1)} %fusion) | data formatting | bytes 1048576 | tf_op jit(solution)/shard_map/stw,pw->stp/dot_general | solution.py:75
  77.7 5.0 %convolution_bitcast_fusion = f32[4,16,256]{1,0,2:T(4,128)S(1)} fusion(f32[32,16,256]{0,1,2:T(8,128)} %copy.22, f32[32,4,256]{0,1,2:T(4,128)S(1)} %copy.23), kind=kOutput, calls=%fused_computation.5 | convolution fusion | flops 6291456 | bytes 720896 | tf_op jit(solution)/shard_map/srp,stp->rtp/dot_general | solution.py:76
  82.7 0.2 copy.24
  82.9 0.7 fusion.2
  (20 shorter events, 0.2 us)
Async XLA Ops:
  0.0 9.8 %copy-start = (bf16[16,16,4096]{2,1,0:T(8,128)(2,1)S(1)}, bf16[16,16,4096]{2,1,0:T(8,128)(2,1)}, u32[]{:S(2)}) copy-start(bf16[16,16,4096]{2,1,0:T(8,128)(2,1)} %param.9) | copy-start | bytes 6291460
  4.7 12.5 %all-to-all-start.1 = ((bf16[8,4,16]{2,1,0:T(4,128)(2,1)}), bf16[8,4,16]{2,1,0:T(4,128)(2,1)S(1)}, u32[]{:S(2)}, u32[]{:S(2)}) async-start(bf16[8,4,16]{2,1,0:T(4,128)(2,1)} %select_convert_fusion), calls=%async_computation.1 | async-start | bytes 16384 | tf_op jit(solution)/shard_map/all_to_all | solution.py:47
  17.1 4.7 %copy-start.1 = (bf16[64,4096]{1,0:T(8,128)(2,1)S(1)}, bf16[64,4096]{1,0:T(8,128)(2,1)}, u32[]{:S(2)}) copy-start(bf16[64,4096]{1,0:T(8,128)(2,1)} %param.10) | copy-start | bytes 1572868
  17.1 53.8 %all-to-all-start = ((bf16[32,16,4096]{2,1,0:T(8,128)(2,1)}), bf16[32,16,4096]{2,1,0:T(8,128)(2,1)}, u32[]{:S(2)}, u32[]{:S(2)}) async-start(bf16[32,16,4096]{2,1,0:T(8,128)(2,1)} %broadcast_select_fusion), calls=%async_computation | async-start | bytes 8388608 | tf_op jit(solution)/shard_map/all_to_all | solution.py:46
  21.8 6.4 %copy-start.2 = (f32[1200]{0:T(1024)S(1)}, f32[1200]{0:T(1024)}, u32[]{:S(2)}) copy-start(f32[1200]{0:T(1024)} %param.15) | copy-start | bytes 14404
  21.8 6.4 %copy-start.3 = (s32[256]{0:T(256)S(1)}, s32[256]{0:T(256)}, u32[]{:S(2)}) copy-start(s32[256]{0:T(256)} %param.16) | copy-start | bytes 3076
  21.9 6.4 %copy-start.4 = (s32[256]{0:T(256)S(1)}, s32[256]{0:T(256)}, u32[]{:S(2)}) copy-start(s32[256]{0:T(256)} %param.17) | copy-start | bytes 3076
  21.9 16.7 %collective-permute-start = (bf16[64,4096]{1,0:T(8,128)(2,1)S(1)}, bf16[64,4096]{1,0:T(8,128)(2,1)}, u32[]{:S(2)}, u32[]{:S(2)}) collective-permute-start(bf16[64,4096]{1,0:T(8,128)(2,1)S(1)} %copy-done.1), channel_id=1, source_target_pairs={{0,8},{8,16},{16,24},{24,0},{1,9},{9,17},{17,25},{25,1},{2,10},{10... | collective-permute-start | bytes 1572872 | tf_op jit(solution)/shard_map/ppermute | solution.py:57
  23.5 25.4 %collective-permute-start.1 = (bf16[64,4096]{1,0:T(8,128)(2,1)S(1)}, bf16[64,4096]{1,0:T(8,128)(2,1)}, u32[]{:S(2)}, u32[]{:S(2)}) collective-permute-start(bf16[64,4096]{1,0:T(8,128)(2,1)S(1)} %copy-done.1), channel_id=1, source_target_pairs={{0,24},{8,0},{16,8},{24,16},{1,25},{9,1},{17,9},{25,17},{2,26},{10... | collective-permute-start | bytes 1572872 | tf_op jit(solution)/shard_map/ppermute | solution.py:60
  38.6 22.0 %collective-permute-start.2 = (bf16[64,4096]{1,0:T(8,128)(2,1)}, bf16[64,4096]{1,0:T(8,128)(2,1)S(1)}, u32[]{:S(2)}, u32[]{:S(2)}) collective-permute-start(bf16[64,4096]{1,0:T(8,128)(2,1)} %collective-permute-done), channel_id=1, source_target_pairs={{0,8},{8,16},{16,24},{24,0},{1,9},{9,17},{17,25},{25,1},{2,10},{10... | collective-permute-start | bytes 1572872 | tf_op jit(solution)/shard_map/ppermute | solution.py:57
  77.7 5.2 %copy-start.5 = (f32[64]{0:T(128)S(1)}, f32[64]{0:T(128)}, u32[]{:S(2)}) copy-start(f32[64]{0:T(128)} %param.14) | copy-start | bytes 772
